TPU v7x, 32 devices: a whole 2x2x4 slice. The times are simulated.
32 devices in a mesh: groups: 1, ctx: 16 (over z, y, x), tp: 1, dp: 2 (over core).
Axes of the slice: x: 2, y: 2, z: 4, core: 2. Of those that a mesh axis runs over, the one named last changes fastest.
Arguments:
- queries: bfloat16 [16384, 4096], P(('groups', 'ctx', 'dp'), 'tp'), may hold values from -128 to 128
- keys: bfloat16 [16384, 512], P(('groups', 'ctx', 'dp'), 'tp'), may hold values from -12 to 12
- values: bfloat16 [16384, 512], P(('groups', 'ctx', 'dp'), 'tp'), may hold values from -8 to 8
- doc_ids: int32 [16384], P(('groups', 'ctx', 'dp')), may hold values from 0 to 63, never falling along the last dimension, each value on 1 to 2048 neighbouring positions
- clip_limits: int32 [4096], P('tp'), may hold values from 256 to 2048
- out_weight: bfloat16 [4096, 8192], P('tp', ('ctx', 'dp')), may hold values from -0.09375 to 0.09375
Outputs:
- attended: bfloat16 [16384, 8192], P(('groups', 'ctx', 'dp'), 'tp')
Inputs may be any that keep to these rules, and one draw needn't show every extreme that they name: `doc_ids`: document numbers never fall along the window; every document holds at most 2048 tokens, and one holds exactly 2048.
All inputs are finite; a program needn't handle non-finite values.
Results may differ from a plain program's by a relative error of at most 0.0095.
Values may be sent and summed in bfloat16 or wider, within the bound.
No kernel may reach another device: no remote copies, remote signals or barrier semaphores. Data moves between devices by JAX's collectives and lax.ppermute only.
A program may use at most 384 MiB of HBM per device.

v0:
```python
import jax
import jax.numpy as jnp
from jax import lax
from jax.sharding import PartitionSpec as P

HD = 128
REACH = 4


neg_big = -1e30
unit_scale = 1024.0


def passed_along(block, axis, distance):
    devices = range(lax.axis_size(axis))
    route = [(i - distance, i) for i in devices if i - distance in devices]
    return lax.ppermute(block, axis, route)


def block_update(
    state, q_split, query_doc, query_pos, key_block, value_block, key_doc, key_location
):
    row_best, row_total, weighted = state
    scores = jnp.einsum(
        "tkge,jke->kgtj", q_split, key_block, preferred_element_type=jnp.float32
    ) * (1.0 / HD**0.5)
    visible = (
        (key_doc[None, :] == query_doc[:, None])
        & (key_location[None, :] <= query_pos[:, None])
        & (key_location[None, :] >= 0)
    )
    scores = jnp.where(visible, scores, neg_big)
    new_best = jnp.maximum(row_best, jnp.max(scores, axis=-1))
    powers = jnp.where(visible, jnp.exp(scores - new_best[..., None]), 0.0)
    factor = jnp.exp(row_best - new_best)
    row_total = row_total * factor + jnp.sum(powers, axis=-1)
    weighted = weighted * factor[..., None] + jnp.einsum(
        "kgtj,jke->kgte",
        powers.astype(jnp.bfloat16),
        value_block,
        preferred_element_type=jnp.float32,
    )
    return (new_best, row_total, weighted)


def local(queries, keys, values, doc_ids, clip_limits, out_weight):
    tok_rows = queries.shape[0]
    kv_heads = keys.shape[1] // HD
    q_heads = queries.shape[1] // HD
    per_group = q_heads // kv_heads
    q_split = queries.reshape(tok_rows, kv_heads, per_group, HD)
    shard_index = lax.axis_index(("ctx", "dp"))
    query_pos = shard_index * tok_rows + jnp.arange(tok_rows, dtype=jnp.int32)
    state = (
        jnp.full((kv_heads, per_group, tok_rows), neg_big, jnp.float32),
        jnp.zeros((kv_heads, per_group, tok_rows), jnp.float32),
        jnp.zeros((kv_heads, per_group, tok_rows, HD), jnp.float32),
    )
    state = block_update(
        state,
        q_split,
        doc_ids,
        query_pos,
        keys.reshape(tok_rows, kv_heads, HD),
        values.reshape(tok_rows, kv_heads, HD),
        doc_ids,
        query_pos,
    )
    moving = (keys, values, doc_ids)
    for offset in range(1, REACH + 1):
        moving = passed_along((moving[0], moving[1], moving[2]), ("ctx", "dp"), 1)
        key_block = moving[0].reshape(tok_rows, kv_heads, HD)
        value_block = moving[1].reshape(tok_rows, kv_heads, HD)
        state = block_update(
            state,
            q_split,
            doc_ids,
            query_pos,
            key_block,
            value_block,
            moving[2],
            query_pos - offset * tok_rows,
        )
    row_best, row_total, weighted = state
    context = weighted / row_total[..., None]
    context = jnp.transpose(context, (2, 0, 1, 3)).reshape(tok_rows, q_heads * HD)
    bounds = clip_limits.astype(jnp.float32) / unit_scale
    clipped = jnp.clip(context, -bounds, bounds).astype(jnp.bfloat16)
    head_terms = jnp.dot(
        clipped,
        lax.all_gather(out_weight, ("ctx", "dp"), axis=1, tiled=True),
        preferred_element_type=jnp.float32,
    ).astype(jnp.bfloat16)
    return lax.psum_scatter(
        head_terms.astype(jnp.float32).astype(jnp.bfloat16), "tp", scatter_dimension=1, tiled=True
    )


def solution(mesh):
    placed = (
        P(("groups", "ctx", "dp"), "tp"),
        P(("groups", "ctx", "dp"), "tp"),
        P(("groups", "ctx", "dp"), "tp"),
        P(("groups", "ctx", "dp")),
        P("tp"),
        P("tp", ("ctx", "dp")),
    )
    return jax.shard_map(
        local,
        mesh=mesh,
        in_specs=placed,
        out_specs=P(("groups", "ctx", "dp"), "tp"),
        check_vma=False,
    )
```

profile of v0, /device:TPU:0, one launch (start us, length us, event | category | flops | bytes accessed | tf_op | source)
XLA Modules:
  0.0 461.8 jit_solution(9417896262579718330)
XLA Ops:
  6.5 0.7 all-gather.2.cloned.1.call-update
  7.3 2.4 collective-permute-start
  9.7 1.3 copy.27
  10.9 4.5 collective-permute-start.1
  15.5 2.7 collective-permute-start.2
  18.2 1.3 convert_multiply_fusion
  19.5 0.0 collective-permute-done
  19.5 2.7 collective-permute-start.3
  22.3 0.8 collective-permute-done.3
  23.0 24.3 %collective-permute-start.6 = (s32[512]{0:T(512)S(1)}, s32[512]{0:T(512)S(1)}, u32[]{:S(2)}, u32[]{:S(2)}) collective-permute-start(s32[512]{0:T(512)S(1)} %collective-permute-done.3), channel_id=1, source_target_pairs={{0,1},{1,2},{2,3},{3,4},{4,5},{5,6},{6,7},{7,8},{8,9},{9,10},{10,1... | collective-permute-start | bytes 6152 | tf_op jit(solution)/shard_map/ppermute | solution.py:17
  47.3 0.8 collective-permute-done.6
  48.1 4.4 collective-permute-start.9
  52.5 1.2 reshape.189
  53.8 1.3 copy.61
  55.0 3.5 copy.70
  58.5 0.0 copy-start
  58.5 0.0 collective-permute-done.9
  58.5 2.5 and_and_fusion.4
  61.0 15.0 %fusion = (f32[4,8,512]{2,1,0:T(8,128)S(1)}, f32[4,512,512,8]{2,1,3,0:T(8,128)}) fusion(pred[512,512]{0,1:T(8,128)(4,1)S(1)} %get-tuple-element.18, bf16[512,4,8,128]{3,2,1,0:T(8,128)(2,1)S(1)} %bitcast.247, bf16[512,4,128,1]{2,1,0,3:T(4,128)(2,1)S(1)} %bitcast.255), kind=kOutput, calls=%fused_computation.10 | convolution fusion | flops 2172633088 | bytes 38600704 | tf_op jit(solution)/shard_map/tkge,jke->kgtj/dot_general | solution.py:24
  76.1 0.0 collective-permute-done.1
  76.1 4.5 collective-permute-start.4
  80.6 2.7 collective-permute-start.5
  83.3 15.4 %fusion.1 = (f32[4,8,512]{2,1,0:T(8,128)S(1)}, f32[4,512,512,8]{2,1,3,0:T(8,128)}) fusion(pred[512,512]{0,1:T(8,128)(4,1)S(1)} %get-tuple-element.22, bf16[512,4,128,1]{0,2,3,1:T(8,128)(2,1)S(1)} %bitcast.256, bf16[512,4,8,128]{3,2,1,0:T(8,128)(2,1)S(1)} %bitcast.248), kind=kOutput, calls=%fused_computation.11 | convolution fusion | flops 2172633088 | bytes 38600704 | tf_op jit(solution)/shard_map/tkge,jke->kgtj/dot_general | solution.py:24
  98.7 2.1 copy.30
  100.7 3.7 collective-permute-start.7
  104.4 13.6 %collective-permute-start.8 = (bf16[512,512]{1,0:T(8,128)(2,1)}, bf16[512,512]{1,0:T(8,128)(2,1)}, u32[]{:S(2)}, u32[]{:S(2)}) collective-permute-start(bf16[512,512]{1,0:T(8,128)(2,1)} %collective-permute-done.5), channel_id=1, source_target_pairs={{0,1},{1,2},{2,3},{3,4},{4,5},{5,6},{6,7},{7,8},{8,9},{9,10},{10,1... | collective-permute-start | bytes 1572872 | tf_op jit(solution)/shard_map/ppermute | solution.py:17
  118.0 21.6 %fusion.2 = (f32[4,8,512]{2,1,0:T(8,128)S(1)}, f32[4,512,512,8]{2,1,3,0:T(8,128)}) fusion(pred[512,512]{0,1:T(8,128)(4,1)S(1)} %get-tuple-element.20, bf16[512,4,128,1]{0,2,3,1:T(8,128)(2,1)S(1)} %bitcast.258, bf16[512,4,8,128]{3,2,1,0:T(8,128)(2,1)} %bitcast.249), kind=kOutput, calls=%fused_computation.12 | convolution fusion | flops 2172633088 | bytes 38600704 | tf_op jit(solution)/shard_map/tkge,jke->kgtj/dot_general | solution.py:24
  139.6 2.1 copy.34
  141.7 3.8 collective-permute-start.10
  145.5 6.4 %collective-permute-start.11 = (bf16[512,512]{1,0:T(8,128)(2,1)}, bf16[512,512]{1,0:T(8,128)(2,1)}, u32[]{:S(2)}, u32[]{:S(2)}) collective-permute-start(bf16[512,512]{1,0:T(8,128)(2,1)} %collective-permute-done.8), channel_id=1, source_target_pairs={{0,1},{1,2},{2,3},{3,4},{4,5},{5,6},{6,7},{7,8},{8,9},{9,10},{10,1... | collective-permute-start | bytes 1572872 | tf_op jit(solution)/shard_map/ppermute | solution.py:17
  151.9 21.7 %fusion.3 = (f32[4,8,512]{2,1,0:T(8,128)S(1)}, f32[4,512,512,8]{2,1,3,0:T(8,128)}) fusion(pred[512,512]{0,1:T(8,128)(4,1)S(1)} %get-tuple-element.21, bf16[512,4,128,1]{0,2,3,1:T(8,128)(2,1)S(1)} %bitcast.257, bf16[512,4,8,128]{3,2,1,0:T(8,128)(2,1)} %bitcast.250), kind=kOutput, calls=%fused_computation.13 | convolution fusion | flops 2172633088 | bytes 38600704 | tf_op jit(solution)/shard_map/tkge,jke->kgtj/dot_general | solution.py:24
  173.6 2.1 copy.38
  175.6 2.1 copy.42
  177.7 22.6 %fusion.4 = (f32[4,8,512]{2,1,0:T(8,128)S(1)}, f32[4,512,512,8]{2,1,3,0:T(8,128)}) fusion(pred[512,512]{0,1:T(8,128)(4,1)S(1)} %get-tuple-element.19, bf16[512,4,128,1]{0,2,3,1:T(8,128)(2,1)S(1)} %bitcast.259, bf16[512,4,8,128]{3,2,1,0:T(8,128)(2,1)} %bitcast.251), kind=kOutput, calls=%fused_computation.14 | convolution fusion | flops 2172633088 | bytes 38600704 | tf_op jit(solution)/shard_map/tkge,jke->kgtj/dot_general | solution.py:24
  200.4 18.0 %fusion.5 = f32[4,8,512]{2,1,0:T(8,128)S(1)} fusion(f32[4,512,512,8]{2,1,3,0:T(8,128)} %get-tuple-element.32, f32[4,8,512]{2,1,0:T(8,128)S(1)} %get-tuple-element.15, pred[512,512]{0,1:T(8,128)(4,1)S(1)} %get-tuple-element.18), kind=kLoop, calls=%fused_computation.15 | loop fusion | flops 41926656 | bytes 33947648 | tf_op jit(solution)/shard_map/reduce_sum | solution.py:36
  218.4 17.4 %fusion.7 = f32[4,8,512]{2,1,0:T(8,128)S(1)} fusion(f32[4,512,512,8]{2,1,3,0:T(8,128)} %get-tuple-element.30, f32[4,8,512]{2,1,0:T(8,128)S(1)} %get-tuple-element.12, pred[512,512]{0,1:T(8,128)(4,1)S(1)} %get-tuple-element.22), kind=kLoop, calls=%fused_computation.17 | loop fusion | flops 41926656 | bytes 33947648 | tf_op jit(solution)/shard_map/reduce_sum | solution.py:36
  235.9 8.4 %fusion.9 = f32[4,8,512]{2,1,0:T(8,128)S(1)} fusion(f32[4,512,512,8]{2,1,3,0:T(8,128)S(1)} %bitcast.253, f32[4,8,512]{2,1,0:T(8,128)S(1)} %get-tuple-element.11, pred[512,512]{0,1:T(8,128)(4,1)S(1)} %get-tuple-element.20), kind=kLoop, calls=%fused_computation.19 | loop fusion | flops 41926656 | bytes 33947648 | tf_op jit(solution)/shard_map/reduce_sum | solution.py:36
  244.3 15.5 %fusion.11 = f32[4,8,512]{2,1,0:T(8,128)S(1)} fusion(f32[4,512,512,8]{2,1,3,0:T(8,128)} %get-tuple-element.26, f32[4,8,512]{2,1,0:T(8,128)S(1)} %get-tuple-element.10, pred[512,512]{0,1:T(8,128)(4,1)S(1)} %get-tuple-element.21), kind=kLoop, calls=%fused_computation.21 | loop fusion | flops 41926656 | bytes 33947648 | tf_op jit(solution)/shard_map/reduce_sum | solution.py:36
  259.8 15.6 %fusion.13 = f32[4,8,512]{2,1,0:T(8,128)S(1)} fusion(f32[4,512,512,8]{2,1,3,0:T(8,128)} %get-tuple-element.24, f32[4,8,512]{2,1,0:T(8,128)S(1)} %get-tuple-element.9, pred[512,512]{0,1:T(8,128)(4,1)S(1)} %get-tuple-element.19), kind=kLoop, calls=%fused_computation.23 | loop fusion | flops 41926656 | bytes 33947648 | tf_op jit(solution)/shard_map/reduce_sum | solution.py:36
  275.4 0.8 bitcast_add_fusion.5
  276.2 17.2 %fusion.23 = f32[4,8,512,128]{2,3,1,0:T(8,128)} fusion(bf16[512,4,128,1]{0,2,3,1:T(8,128)(2,1)S(1)} %bitcast.260, f32[4,512,512,8]{2,1,3,0:T(8,128)} %get-tuple-element.32, f32[4,8,512]{2,1,0:T(8,128)S(1)} %get-tuple-element.15, pred[512,512]{0,1:T(8,128)(4,1)S(1)} %get-tuple-element.18), kind=kOutput, calls=%fused_computation.29 | convolution fusion | flops 2189426688 | bytes 42795008 | tf_op jit(solution)/shard_map/kgtj,jke->kgte/dot_general | solution.py:37
  293.3 18.3 %fusion.21 = f32[4,8,512,128]{2,3,1,0:T(8,128)} fusion(bf16[512,4,128,1]{0,2,3,1:T(8,128)(2,1)S(1)} %bitcast.261, f32[4,512,512,8]{2,1,3,0:T(8,128)} %get-tuple-element.30, f32[4,8,512]{2,1,0:T(8,128)S(1)} %get-tuple-element.12, pred[512,512]{0,1:T(8,128)(4,1)S(1)} %get-tuple-element.22), kind=kOutput, calls=%fused_computation.28 | convolution fusion | flops 2189426688 | bytes 42795008 | tf_op jit(solution)/shard_map/kgtj,jke->kgte/dot_general | solution.py:37
  311.6 19.6 %fusion.19 = f32[4,8,512,128]{2,3,1,0:T(8,128)} fusion(bf16[512,4,128,1]{0,2,3,1:T(8,128)(2,1)S(1)} %bitcast.262, f32[4,512,512,8]{2,1,3,0:T(8,128)} %get-tuple-element.28, f32[4,8,512]{2,1,0:T(8,128)S(1)} %get-tuple-element.11, pred[512,512]{0,1:T(8,128)(4,1)S(1)} %get-tuple-element.20), kind=kOutput, calls=%fused_computation.27 | convolution fusion | flops 2189426688 | bytes 42795008 | tf_op jit(solution)/shard_map/kgtj,jke->kgte/dot_general | solution.py:37
  331.2 17.8 %fusion.17 = f32[4,8,512,128]{2,3,1,0:T(8,128)} fusion(bf16[512,4,128,1]{0,2,3,1:T(8,128)(2,1)S(1)} %bitcast.263, f32[4,512,512,8]{2,1,3,0:T(8,128)} %get-tuple-element.26, f32[4,8,512]{2,1,0:T(8,128)S(1)} %get-tuple-element.10, pred[512,512]{0,1:T(8,128)(4,1)S(1)} %get-tuple-element.21), kind=kOutput, calls=%fused_computation.26 | convolution fusion | flops 2189426688 | bytes 42795008 | tf_op jit(solution)/shard_map/kgtj,jke->kgte/dot_general | solution.py:37
  349.0 24.8 %fusion.32 = bf16[512,4,8,128]{0,3,2,1:T(8,128)(2,1)S(1)} fusion(f32[4,8,512,128]{2,3,1,0:T(8,128)} %fusion.17, f32[4,8,512,128]{2,3,1,0:T(8,128)} %fusion.19, f32[4,8,512,128]{2,3,1,0:T(8,128)} %fusion.21, f32[4,8,512,128]{2,3,1,0:T(8,128)} %fusion.23, f32[512,4,8]{0,2,1:T(8,128)S(1)} %get-tuple-element.5, f32[512,4,8]{0,2,1:T(8,128)S(1)} %copy-done.5, ...), kind=kOutput, calls=%fused_computation.40 | convolution fusion | flops 2212495360 | bytes 72548352 | tf_op jit(solution)/shard_map/kgtj,jke->kgte/dot_general | solution.py:37
  373.9 2.9 fusion.31
  376.8 33.6 %all-gather.2.cloned.1.call-done = bf16[4096,8192]{1,0:T(8,128)(2,1)} async-done(((bf16[4096,256]{1,0:T(8,128)(2,1)}), bf16[4096,8192]{1,0:T(8,128)(2,1)}) %all-gather.2.cloned.1.call-update) | async-done | bytes 67108880 | tf_op jit(solution)/shard_map/all_gather | solution.py:91
  410.4 44.4 %convolution_convert_fusion = bf16[512,8192]{1,0:T(8,128)(2,1)} fusion(bf16[512,4096]{0,1:T(8,128)(2,1)} %fusion.31, bf16[4096,8192]{1,0:T(8,128)(2,1)} %all-gather.2.cloned.1.call-done), kind=kOutput, calls=%fused_computation.35 | convolution fusion | flops 34363932672 | bytes 79691776 | tf_op jit(solution)/shard_map/dot_general | solution.py:89
  (51 shorter events, 0.2 us)
Async XLA Ops:
  6.5 403.8 %all-gather.2.cloned.1.call-start = ((), (), s32[]{:S(2)}) async-start(), calls=%async_computation | async-start | bytes 69206016 | tf_op jit(solution)/shard_map/all_gather | solution.py:91
  7.3 12.3 %collective-permute-start = (s32[512]{0:T(512)}, s32[512]{0:T(512)S(1)}, u32[]{:S(2)}, u32[]{:S(2)}) collective-permute-start(s32[512]{0:T(512)} %param.9), channel_id=1, source_target_pairs={{0,1},{1,2},{2,3},{3,4},{4,5},{5,6},{6,7},{7,8},{8,9},{9,10},{10,1... | collective-permute-start | bytes 6152 | tf_op jit(solution)/shard_map/ppermute | solution.py:17
  10.9 65.2 %collective-permute-start.1 = (bf16[512,512]{0,1:T(8,128)(2,1)S(1)}, bf16[512,512]{0,1:T(8,128)(2,1)S(1)}, u32[]{:S(2)}, u32[]{:S(2)}) collective-permute-start(bf16[512,512]{0,1:T(8,128)(2,1)S(1)} %copy.27), channel_id=1, source_target_pairs={{0,1},{1,2},{2,3},{3,4},{4,5},{5,6},{6,7},{7,8},{8,9},{9,10},{10,1... | collective-permute-start | bytes 1572872 | tf_op jit(solution)/shard_map/ppermute | solution.py:17
  15.5 65.1 %collective-permute-start.2 = (bf16[512,512]{1,0:T(8,128)(2,1)}, bf16[512,512]{1,0:T(8,128)(2,1)}, u32[]{:S(2)}, u32[]{:S(2)}) collective-permute-start(bf16[512,512]{1,0:T(8,128)(2,1)} %param.8), channel_id=1, source_target_pairs={{0,1},{1,2},{2,3},{3,4},{4,5},{5,6},{6,7},{7,8},{8,9},{9,10},{10,1... | collective-permute-start | bytes 1572872 | tf_op jit(solution)/shard_map/ppermute | solution.py:17
  19.5 3.5 collective-permute-start.3
  23.0 25.1 %collective-permute-start.6 = (s32[512]{0:T(512)S(1)}, s32[512]{0:T(512)S(1)}, u32[]{:S(2)}, u32[]{:S(2)}) collective-permute-start(s32[512]{0:T(512)S(1)} %collective-permute-done.3), channel_id=1, source_target_pairs={{0,1},{1,2},{2,3},{3,4},{4,5},{5,6},{6,7},{7,8},{8,9},{9,10},{10,1... | collective-permute-start | bytes 6152 | tf_op jit(solution)/shard_map/ppermute | solution.py:17
  48.1 10.4 %collective-permute-start.9 = (s32[512]{0:T(512)S(1)}, s32[512]{0:T(512)S(1)}, u32[]{:S(2)}, u32[]{:S(2)}) collective-permute-start(s32[512]{0:T(512)S(1)} %collective-permute-done.6), channel_id=1, source_target_pairs={{0,1},{1,2},{2,3},{3,4},{4,5},{5,6},{6,7},{7,8},{8,9},{9,10},{10,1... | collective-permute-start | bytes 6152 | tf_op jit(solution)/shard_map/ppermute | solution.py:17
  58.5 24.8 %copy-start = (bf16[64,8,32,128]{3,2,1,0:T(8,128)(2,1)}, bf16[64,8,32,128]{3,2,1,0:T(8,128)(2,1)S(1)}, u32[]{:S(2)}) copy-start(bf16[64,8,32,128]{3,2,1,0:T(8,128)(2,1)S(1)} %copy.70) | copy-start | bytes 12582916
  76.1 24.6 %collective-permute-start.4 = (bf16[512,512]{0,1:T(8,128)(2,1)S(1)}, bf16[512,512]{0,1:T(8,128)(2,1)S(1)}, u32[]{:S(2)}, u32[]{:S(2)}) collective-permute-start(bf16[512,512]{0,1:T(8,128)(2,1)S(1)} %collective-permute-done.1), channel_id=1, source_target_pairs={{0,1},{1,2},{2,3},{3,4},{4,5},{5,6},{6,7},{7,8},{8,9},{9,10},{10,1... | collective-permute-start | bytes 1572872 | tf_op jit(solution)/shard_map/ppermute | solution.py:17
  80.6 23.8 %collective-permute-start.5 = (bf16[512,512]{1,0:T(8,128)(2,1)}, bf16[512,512]{1,0:T(8,128)(2,1)}, u32[]{:S(2)}, u32[]{:S(2)}) collective-permute-start(bf16[512,512]{1,0:T(8,128)(2,1)} %collective-permute-done.2), channel_id=1, source_target_pairs={{0,1},{1,2},{2,3},{3,4},{4,5},{5,6},{6,7},{7,8},{8,9},{9,10},{10,1... | collective-permute-start | bytes 1572872 | tf_op jit(solution)/shard_map/ppermute | solution.py:17
  100.7 40.9 %collective-permute-start.7 = (bf16[512,512]{0,1:T(8,128)(2,1)S(1)}, bf16[512,512]{0,1:T(8,128)(2,1)S(1)}, u32[]{:S(2)}, u32[]{:S(2)}) collective-permute-start(bf16[512,512]{0,1:T(8,128)(2,1)S(1)} %collective-permute-done.4), channel_id=1, source_target_pairs={{0,1},{1,2},{2,3},{3,4},{4,5},{5,6},{6,7},{7,8},{8,9},{9,10},{10,1... | collective-permute-start | bytes 1572872 | tf_op jit(solution)/shard_map/ppermute | solution.py:17
  104.4 41.1 %collective-permute-start.8 = (bf16[512,512]{1,0:T(8,128)(2,1)}, bf16[512,512]{1,0:T(8,128)(2,1)}, u32[]{:S(2)}, u32[]{:S(2)}) collective-permute-start(bf16[512,512]{1,0:T(8,128)(2,1)} %collective-permute-done.5), channel_id=1, source_target_pairs={{0,1},{1,2},{2,3},{3,4},{4,5},{5,6},{6,7},{7,8},{8,9},{9,10},{10,1... | collective-permute-start | bytes 1572872 | tf_op jit(solution)/shard_map/ppermute | solution.py:17
  141.7 36.1 %collective-permute-start.10 = (bf16[512,512]{0,1:T(8,128)(2,1)S(1)}, bf16[512,512]{0,1:T(8,128)(2,1)S(1)}, u32[]{:S(2)}, u32[]{:S(2)}) collective-permute-start(bf16[512,512]{0,1:T(8,128)(2,1)S(1)} %collective-permute-done.7), channel_id=1, source_target_pairs={{0,1},{1,2},{2,3},{3,4},{4,5},{5,6},{6,7},{7,8},{8,9},{9,10},{10,1... | collective-permute-start | bytes 1572872 | tf_op jit(solution)/shard_map/ppermute | solution.py:17
  145.5 30.2 %collective-permute-start.11 = (bf16[512,512]{1,0:T(8,128)(2,1)}, bf16[512,512]{1,0:T(8,128)(2,1)}, u32[]{:S(2)}, u32[]{:S(2)}) collective-permute-start(bf16[512,512]{1,0:T(8,128)(2,1)} %collective-permute-done.8), channel_id=1, source_target_pairs={{0,1},{1,2},{2,3},{3,4},{4,5},{5,6},{6,7},{7,8},{8,9},{9,10},{10,1... | collective-permute-start | bytes 1572872 | tf_op jit(solution)/shard_map/ppermute | solution.py:17
  200.4 35.4 %slice-start = ((s8[33554432]{0:T(1024)(128)(4,1)}), s8[4194304]{0:T(1024)(128)(4,1)S(1)}, s32[]{:S(2)}) async-start(s8[33554432]{0:T(1024)(128)(4,1)} %bitcast.252), calls=%async_computation.1 | async-start | bytes 8388608
  200.4 35.4 %slice-start.1 = ((s8[33554432]{0:T(1024)(128)(4,1)}), s8[4194304]{0:T(1024)(128)(4,1)S(1)}, s32[]{:S(2)}) async-start(s8[33554432]{0:T(1024)(128)(4,1)} %bitcast.252), calls=%async_computation.2 | async-start | bytes 8388608
  200.4 35.4 %slice-start.2 = ((s8[33554432]{0:T(1024)(128)(4,1)}), s8[4194304]{0:T(1024)(128)(4,1)S(1)}, s32[]{:S(2)}) async-start(s8[33554432]{0:T(1024)(128)(4,1)} %bitcast.252), calls=%async_computation.3 | async-start | bytes 8388608
  200.4 35.4 %slice-start.3 = ((s8[33554432]{0:T(1024)(128)(4,1)}), s8[4194304]{0:T(1024)(128)(4,1)S(1)}, s32[]{:S(2)}) async-start(s8[33554432]{0:T(1024)(128)(4,1)} %bitcast.252), calls=%async_computation.4 | async-start | bytes 8388608
  218.4 17.4 %slice-start.4 = ((s8[33554432]{0:T(1024)(128)(4,1)}), s8[4194304]{0:T(1024)(128)(4,1)S(1)}, s32[]{:S(2)}) async-start(s8[33554432]{0:T(1024)(128)(4,1)} %bitcast.252), calls=%async_computation.5 | async-start | bytes 8388608
  218.4 17.4 %slice-start.5 = ((s8[33554432]{0:T(1024)(128)(4,1)}), s8[4194304]{0:T(1024)(128)(4,1)S(1)}, s32[]{:S(2)}) async-start(s8[33554432]{0:T(1024)(128)(4,1)} %bitcast.252), calls=%async_computation.6 | async-start | bytes 8388608
  218.4 17.4 %slice-start.6 = ((s8[33554432]{0:T(1024)(128)(4,1)}), s8[4194304]{0:T(1024)(128)(4,1)S(1)}, s32[]{:S(2)}) async-start(s8[33554432]{0:T(1024)(128)(4,1)} %bitcast.252), calls=%async_computation.7 | async-start | bytes 8388608
  218.4 17.4 %slice-start.7 = ((s8[33554432]{0:T(1024)(128)(4,1)}), s8[4194304]{0:T(1024)(128)(4,1)S(1)}, s32[]{:S(2)}) async-start(s8[33554432]{0:T(1024)(128)(4,1)} %bitcast.252), calls=%async_computation.8 | async-start | bytes 8388608
  275.4 17.9 %copy-start.1 = (bf16[512,512]{0,1:T(8,128)(2,1)S(1)}, bf16[512,512]{0,1:T(8,128)(2,1)}, u32[]{:S(2)}) copy-start(bf16[512,512]{0,1:T(8,128)(2,1)} %copy.30) | copy-start | bytes 1572868
  293.3 18.3 %copy-start.2 = (bf16[512,512]{0,1:T(8,128)(2,1)S(1)}, bf16[512,512]{0,1:T(8,128)(2,1)}, u32[]{:S(2)}) copy-start(bf16[512,512]{0,1:T(8,128)(2,1)} %copy.34) | copy-start | bytes 1572868
  311.6 19.6 %copy-start.3 = (bf16[512,512]{0,1:T(8,128)(2,1)S(1)}, bf16[512,512]{0,1:T(8,128)(2,1)}, u32[]{:S(2)}) copy-start(bf16[512,512]{0,1:T(8,128)(2,1)} %copy.38) | copy-start | bytes 1572868
  331.2 17.8 %copy-start.4 = (bf16[512,512]{0,1:T(8,128)(2,1)S(1)}, bf16[512,512]{0,1:T(8,128)(2,1)}, u32[]{:S(2)}) copy-start(bf16[512,512]{0,1:T(8,128)(2,1)} %copy.42) | copy-start | bytes 1572868
  331.2 17.8 %copy-start.5 = (f32[512,4,8]{0,2,1:T(8,128)S(1)}, f32[512,4,8]{0,2,1:T(8,128)}, u32[]{:S(2)}) copy-start(f32[512,4,8]{0,2,1:T(8,128)} %get-tuple-element.8) | copy-start | bytes 196612
  331.2 17.8 %copy-start.6 = (f32[512,4,8]{0,2,1:T(8,128)S(1)}, f32[512,4,8]{0,2,1:T(8,128)}, u32[]{:S(2)}) copy-start(f32[512,4,8]{0,2,1:T(8,128)} %get-tuple-element.13) | copy-start | bytes 196612
  331.2 17.8 %copy-start.7 = (f32[512,4,8]{0,2,1:T(8,128)S(1)}, f32[512,4,8]{0,2,1:T(8,128)}, u32[]{:S(2)}) copy-start(f32[512,4,8]{0,2,1:T(8,128)} %get-tuple-element.14) | copy-start | bytes 196612
  349.0 24.9 %copy-start.8 = (bf16[4096]{0:T(1024)(128)(2,1)S(1)}, bf16[4096]{0:T(1024)(128)(2,1)}, u32[]{:S(2)}) copy-start(bf16[4096]{0:T(1024)(128)(2,1)} %get-tuple-element.16) | copy-start | bytes 24580
  349.0 24.9 %copy-start.9 = (bf16[4096]{0:T(1024)(128)(2,1)S(1)}, bf16[4096]{0:T(1024)(128)(2,1)}, u32[]{:S(2)}) copy-start(bf16[4096]{0:T(1024)(128)(2,1)} %get-tuple-element.17) | copy-start | bytes 24580
Sparse Core Ops, SparseCore 0:
  8.8 401.4 all-gather.1
where the time goes:
time: 470 us; the launch traced here: 462 us
  matrix products  238 us (51%)
  other arithmetic  82.4 us (18%)
  starting transfers between devices  75.7 us (16%)
  waiting for transfers between devices  35.9 us (8%)
  local copies, waits for them, and re-layouts  15.5 us (3%)
  between operations  14 us (3%)
    dot_general x5, matrix products, block_update(): jnp.einsum('kgtj,jke->kgte', powers.astype(jnp.bfloat16), value_block, pr...  97.6 us
    dot_general x5, matrix products, block_update(): jnp.einsum('tkge,jke->kgtj', q_split, key_block, preferred_element_type=j...  96.3 us
    ppermute x12, starting transfers between devices, passed_along(): return lax.ppermute(block, axis, route)  75.7 us
    reduce_sum x5, other arithmetic, block_update(): row_total = row_total * factor + jnp.sum(powers, axis=-1)  74.8 us
    dot_general x1, matrix products, local(): jnp.dot(clipped, lax.all_gather(out_weight, ('ctx', 'dp'), axis=1, tiled=...  44.4 us
    all_gather x1, waiting for transfers between devices, local(): lax.all_gather(out_weight, ('ctx', 'dp'), axis=1, tiled=True)  33.6 us
  transfers between devices with their start and end apart: 13, of which 3 were waited for; matrix products, arithmetic and copies ran while one was open for 63% of the time, Pallas kernels for 0%

commit v1 on v0

v1 whole, which is shorter than its diff:
```python
import functools

import jax
import jax.numpy as jnp
from jax import lax
from jax.experimental import pallas as pl
from jax.experimental.pallas import tpu as pltpu
from jax.sharding import PartitionSpec as P


HD = 128
Q_TILE = 256
K_TILE = 512
neg_big = -1e30
unit_scale = 1024.0
LOG2E = 1.4426950408889634


def attend_kernel(
    bounds_ref, q_ref, start_ref, clip_ref, *refs, heads, tok, q_tile, k_tile
):
    shards = refs[:12]
    o_ref, k_scr, v_scr, m_scr, a_scr = refs[12:]
    qi = pl.program_id(1)
    own_side = bounds_ref[0]

    @pl.when((qi == 0) & (pl.program_id(0) == 0))
    def _():
        v_scr[:, :, HD:] = jnp.ones((6, tok, HD), jnp.bfloat16)

    @pl.when(qi == 0)
    def _():
        for spot in range(6):
            k_scr[spot] = shards[2 * spot][:tok]
            v_scr[spot, :, :HD] = shards[2 * spot + 1][:tok]

    scale = LOG2E / HD**0.5
    q_first = (4 + own_side) * tok + qi * q_tile
    per_shard = tok // k_tile
    last = q_first // k_tile
    first = bounds_ref[1 + qi]
    m_scr[...] = jnp.full_like(m_scr, neg_big)
    a_scr[...] = jnp.zeros_like(a_scr)
    start_col = start_ref[...]
    row_pos = q_first + lax.broadcasted_iota(jnp.int32, (q_tile, k_tile), 0)

    def step(i, carry):
        blk = last - i
        shard = blk // per_shard
        spot = lax.rem(shard + own_side, 2) * 3 + shard // 2
        rows = pl.ds(pl.multiple_of(lax.rem(blk, per_shard) * k_tile, k_tile), k_tile)
        k_blk = k_scr[spot, rows]
        v_blk = v_scr[spot, rows]
        key_pos = blk * k_tile + lax.broadcasted_iota(
            jnp.int32, (q_tile, k_tile), 1
        )
        seen = (key_pos >= start_col) & (key_pos <= row_pos)
        bias = jnp.where(seen, 0.0, neg_big)
        for h in range(heads):
            s = lax.dot_general(
                q_ref[:, h * HD : (h + 1) * HD],
                k_blk,
                (((1,), (1,)), ((), ())),
                preferred_element_type=jnp.float32,
            )
            s = s + bias
            m_old = m_scr[h]
            m_new = jnp.maximum(m_old, jnp.max(s, axis=-1, keepdims=True))
            m_scr[h] = m_new
            wide = jnp.concatenate([m_new] * (k_tile // HD), axis=1)
            p = jnp.exp2((s - wide) * scale).astype(jnp.bfloat16)
            alpha = jnp.exp2((m_old - m_new) * scale)
            a_scr[h] = a_scr[h] * jnp.concatenate([alpha, alpha], axis=1) + jnp.dot(
                p, v_blk, preferred_element_type=jnp.float32
            )
        return carry

    lax.fori_loop(0, last - first + 1, step, 0)
    for h in range(heads):
        ctx = a_scr[h, :, :HD] / a_scr[h, :, HD:]
        lim = clip_ref[:, h * HD : (h + 1) * HD].astype(jnp.float32) / unit_scale
        ctx = jnp.minimum(jnp.maximum(ctx, -lim), lim)
        o_ref[:, h * HD : (h + 1) * HD] = ctx.astype(o_ref.dtype)


def attend(bounds, queries, start, limits, shards, g0, groups, kv_heads):
    tok = queries.shape[0]
    heads = queries.shape[1] // HD // kv_heads
    q_tile, k_tile = min(Q_TILE, tok), min(K_TILE, tok)
    width = heads * HD
    shard_specs, shard_args = [], []
    for a in shards:
        rows = a.shape[0]
        shard_args += [a, a]
        shard_specs += [
            pl.BlockSpec((rows, HD), lambda g, i, *_: (0, g0 + g)),
            pl.BlockSpec((rows, HD), lambda g, i, *_: (0, kv_heads + g0 + g)),
        ]
    return pl.pallas_call(
        functools.partial(
            attend_kernel, heads=heads, tok=tok, q_tile=q_tile, k_tile=k_tile
        ),
        out_shape=jax.ShapeDtypeStruct((tok, groups * width), jnp.bfloat16),
        grid_spec=pltpu.PrefetchScalarGridSpec(
            num_scalar_prefetch=1,
            grid=(groups, tok // q_tile),
            in_specs=[
                pl.BlockSpec((q_tile, width), lambda g, i, *_: (i, g0 + g)),
                pl.BlockSpec((q_tile, 1), lambda g, i, *_: (i, 0)),
                pl.BlockSpec((1, width), lambda g, i, *_: (0, g0 + g)),
            ]
            + shard_specs,
            out_specs=pl.BlockSpec((q_tile, width), lambda g, i, *_: (i, g)),
            scratch_shapes=[
                pltpu.VMEM((6, tok, HD), jnp.bfloat16),
                pltpu.VMEM((6, tok, 2 * HD), jnp.bfloat16),
                pltpu.VMEM((heads, q_tile, HD), jnp.float32),
                pltpu.VMEM((heads, q_tile, 2 * HD), jnp.float32),
            ],
        ),
        compiler_params=pltpu.CompilerParams(vmem_limit_bytes=40 << 20),
        cost_estimate=pl.CostEstimate(
            flops=4 * tok * width * groups * 4 * tok,
            transcendentals=tok * heads * groups * 4 * tok,
            bytes_accessed=4 * tok * width * groups,
        ),
    )(bounds, queries, start, limits, *shard_args)


def project_kernel(idx_ref, *refs, n_ctx, layout, aliased, tok, cols):
    own = refs[:n_ctx]
    partner = refs[n_ctx : 2 * n_ctx]
    n_pieces = sum(len(p) for p in layout)
    pieces = refs[2 * n_ctx : 2 * n_ctx + n_pieces]
    rest = refs[2 * n_ctx + n_pieces + (1 if aliased else 0) :]
    out_ref, send_ref, c_buf, w_buf, o_buf, c_sem, w_sem, o_sem = rest
    width = own[0].shape[1]
    ctx_copies = []
    for side, group in enumerate((own, partner)):
        for g, ref in enumerate(group):
            ctx_copies.append(
                pltpu.make_async_copy(
                    ref,
                    c_buf.at[side, :, pl.ds(g * width, width)],
                    c_sem.at[side * n_ctx + g],
                )
            )
    weight_copies = []
    at = 0
    for s, plan in enumerate(layout):
        mine = []
        for src, row, rows in plan:
            ref = pieces[at] if src is None else pieces[at].at[src]
            mine.append(
                pltpu.make_async_copy(
                    ref, w_buf.at[s, pl.ds(row, rows)], w_sem.at[at]
                )
            )
            at += 1
        weight_copies.append(mine)
    for cp in ctx_copies[:n_ctx] + weight_copies[0]:
        cp.start()
    for cp in ctx_copies[n_ctx:]:
        cp.start()
    for mine in weight_copies[1:]:
        for cp in mine:
            cp.start()
    out_copies = []
    for s in range(len(layout)):
        if s == 0:
            for cp in ctx_copies:
                cp.wait()
        for cp in weight_copies[s]:
            cp.wait()

        @pl.loop(0, 2)
        def _(side):
            o_buf[s, side] = jnp.dot(
                c_buf[side], w_buf[s], preferred_element_type=jnp.float32
            ).astype(jnp.bfloat16)

        spot = pl.multiple_of(idx_ref[s] * cols, cols)
        for side, dst in enumerate(
            (out_ref.at[:, pl.ds(spot, cols)], send_ref.at[:, pl.ds(s * cols, cols)])
        ):
            cp = pltpu.make_async_copy(
                o_buf.at[s, side], dst, o_sem.at[2 * s + side]
            )
            cp.start()
            out_copies.append(cp)
    for cp in out_copies:
        cp.wait()


def project(idx, own, partner, layout, pieces, out, out_cols, cols):
    tok = own[0].shape[0]
    depth = own[0].shape[1] * len(own)
    n = len(layout)
    aliased = out is not None
    args = [idx, *own, *partner, *pieces] + ([out] if aliased else [])
    hbm = pl.BlockSpec(memory_space=pl.ANY)
    return pl.pallas_call(
        functools.partial(
            project_kernel,
            n_ctx=len(own),
            layout=layout,
            aliased=aliased,
            tok=tok,
            cols=cols,
        ),
        out_shape=(
            jax.ShapeDtypeStruct((tok, out_cols), jnp.bfloat16),
            jax.ShapeDtypeStruct((tok, n * cols), jnp.bfloat16),
        ),
        grid_spec=pltpu.PrefetchScalarGridSpec(
            num_scalar_prefetch=1,
            grid=(1,),
            in_specs=[hbm] * (len(args) - 1),
            out_specs=(hbm, hbm),
            scratch_shapes=[
                pltpu.VMEM((2, tok, depth), jnp.bfloat16),
                pltpu.VMEM((n, depth, cols), jnp.bfloat16),
                pltpu.VMEM((n, 2, tok, cols), jnp.bfloat16),
                pltpu.SemaphoreType.DMA((2 * len(own),)),
                pltpu.SemaphoreType.DMA((len(pieces),)),
                pltpu.SemaphoreType.DMA((2 * n,)),
            ],
        ),
        input_output_aliases={len(args) - 1: 0} if aliased else {},
        compiler_params=pltpu.CompilerParams(vmem_limit_bytes=48 << 20),
        cost_estimate=pl.CostEstimate(
            flops=4 * tok * depth * n * cols,
            transcendentals=0,
            bytes_accessed=2 * depth * (2 * tok + n * cols),
        ),
    )(*args)


def place_kernel(idx_ref, *refs, n_src, per, cols):
    srcs = refs[:n_src]
    out_ref, sem = refs[n_src + 1 :]
    copies = []
    for a in range(n_src):
        for s in range(per[a]):
            at = len(copies)
            spot = pl.multiple_of(idx_ref[at] * cols, cols)
            cp = pltpu.make_async_copy(
                srcs[a].at[:, pl.ds(s * cols, cols)],
                out_ref.at[:, pl.ds(spot, cols)],
                sem.at[at],
            )
            cp.start()
            copies.append(cp)
    for cp in copies:
        cp.wait()


def place(idx, srcs, out, cols):
    per = tuple(a.shape[1] // cols for a in srcs)
    hbm = pl.BlockSpec(memory_space=pl.ANY)
    return pl.pallas_call(
        functools.partial(place_kernel, n_src=len(srcs), per=per, cols=cols),
        out_shape=jax.ShapeDtypeStruct(out.shape, out.dtype),
        grid_spec=pltpu.PrefetchScalarGridSpec(
            num_scalar_prefetch=1,
            grid=(1,),
            in_specs=[
                pl.BlockSpec(a.shape, lambda i, *_: (0, 0)) for a in srcs
            ]
            + [hbm],
            out_specs=hbm,
            scratch_shapes=[pltpu.SemaphoreType.DMA((sum(per),))],
        ),
        input_output_aliases={len(srcs) + 1: 0},
    )(idx, *srcs, out)


def steps(queries, keys, values, doc_ids, clip_limits, out_weight):
    tok = queries.shape[0]
    kv_heads = keys.shape[1] // HD
    kv_cols = 2 * keys.shape[1]
    depth, cols = out_weight.shape
    n_ctx, n_dp = lax.axis_size("ctx"), lax.axis_size("dp")
    out_cols = cols * n_ctx * n_dp
    c, d = lax.axis_index("ctx"), lax.axis_index("dp")
    layers = n_ctx // 4

    def swap(a):
        return lax.ppermute(a, "dp", [(0, 1), (1, 0)])

    def lift(a):
        pairs = [(i, i + 4) for i in range(n_ctx - 4) if i % 4 >= 2]
        return lax.ppermute(a, "ctx", pairs)

    def flip(a, bit):
        return lax.ppermute(a, "ctx", [(i, i ^ bit) for i in range(n_ctx)])

    def rise(a, by):
        return lax.ppermute(
            a, "ctx", [(i, (i + by) % n_ctx) for i in range(n_ctx)]
        )

    doc_rows = jnp.pad(doc_ids.astype(jnp.bfloat16), (0, 16 * kv_cols - tok))
    bundle = jnp.concatenate(
        [
            jnp.concatenate([keys, values], axis=1),
            doc_rows.reshape(16, kv_cols),
        ],
        axis=0,
    )
    below = lift(bundle)
    place_in_layer = lax.rem(c, 4)
    before_2 = flip(jnp.where(place_in_layer >= 2, below, bundle), 2)
    before_1 = flip(jnp.where(place_in_layer % 2 == 1, before_2, bundle), 1)
    mine = (before_2, before_1, bundle)
    theirs = (swap(before_2), swap(before_1), swap(bundle))
    shards = [pltpu.with_memory_space_constraint(a, pltpu.HBM) for a in mine + theirs]

    w = {(0, 0): out_weight}
    w[1, 0] = rise(out_weight, 4)
    w[3, 0] = rise(out_weight, -4)
    w[0, 1] = flip(out_weight, 1)
    w[0, 2] = flip(out_weight, 2)
    w[0, 3] = flip(w[0, 2], 1)
    w[2, 0] = rise(w[1, 0], 4)
    w[1, 1] = flip(w[1, 0], 1)
    w[1, 2] = flip(w[1, 0], 2)
    w[2, 1] = flip(w[2, 0], 1)
    w[2, 2] = flip(w[2, 0], 2)
    w[3, 1] = flip(w[3, 0], 1)
    w[3, 2] = flip(w[3, 0], 2)
    w[1, 3] = rise(w[0, 3], 4)
    w[2, 3] = rise(w[1, 3], 4)
    w[3, 3] = flip(w[3, 1], 2)

    def docs_of(a, valid):
        ids = a[tok:].reshape(-1)[:tok].astype(jnp.int32)
        return jnp.where(valid, ids, -1)

    window_docs = jnp.concatenate(
        [
            docs_of(a, c >= age)
            for side in (mine, theirs)
            for age, a in zip((2, 1, 0), side)
        ]
    )
    start = jnp.sum(
        (window_docs[None, :] < doc_ids[:, None]).astype(jnp.int32),
        axis=1,
        keepdims=True,
    )
    q_tile, k_tile = min(Q_TILE, tok), min(K_TILE, tok)
    bounds = jnp.concatenate(
        [d[None].astype(jnp.int32), start[::q_tile, 0] // k_tile]
    )
    limits = clip_limits.reshape(1, -1)

    groups = 1
    own, partner = [], []
    for g0 in range(0, kv_heads, groups):
        own.append(
            attend(
                bounds, queries, start, limits, shards, g0, groups, kv_heads
            )
        )
        partner.append(swap(own[-1]))

    def columns_of(shards, side):
        spots = [
            (lax.rem(c // 4 - layer + layers, layers) * 4 + (lax.rem(c, 4) ^ f)) * n_dp
            + side
            for layer, f in shards
        ]
        return jnp.stack(spots).astype(jnp.int32)

    def placed(out, first, last):
        shards = [s for part in PARTS[first:last] for s in part]
        return place(columns_of(shards, 1 - d), arrived[first:last], out, cols)

    out = None
    arrived = []
    for n, part in enumerate(PARTS):
        if n == len(PARTS) - 1:
            out = placed(out, 0, n)
        out, sent = project(
            columns_of(part, d),
            own,
            partner,
            tuple(((None, 0, depth),) for _ in part),
            [w[s] for s in part],
            out,
            out_cols,
            cols,
        )
        arrived.append(swap(sent))
    out = placed(out, len(PARTS) - 1, len(PARTS))
    if lax.axis_size("tp") > 1:
        out = lax.psum_scatter(out, "tp", scatter_dimension=1, tiled=True)
    return out


PARTS = (
    ((0, 0), (0, 1), (0, 2), (0, 3)),
    ((1, 0), (1, 1), (1, 2)),
    ((3, 0), (3, 1), (3, 2)),
    ((2, 0), (1, 3), (2, 2)),
    ((2, 1), (2, 3)),
    ((3, 3),),
)


def solution(mesh):
    placed = (
        P(("groups", "ctx", "dp"), "tp"),
        P(("groups", "ctx", "dp"), "tp"),
        P(("groups", "ctx", "dp"), "tp"),
        P(("groups", "ctx", "dp")),
        P("tp"),
        P("tp", ("ctx", "dp")),
    )
    return jax.shard_map(
        steps,
        mesh=mesh,
        in_specs=placed,
        out_specs=P(("groups", "ctx", "dp"), "tp"),
        check_vma=False,
    )
```

time: 470 us -> 402 us (0.86); the launches traced: 462 us -> 402 us
  matrix products: 238 us -> 0 us
  waiting for transfers between devices: 35.9 us -> 194 us
  Pallas kernels: 0 us -> 107 us
  other arithmetic: 82.4 us -> 6.06 us
  between operations: 14 us -> 0.6 us
  starting transfers between devices: 75.7 us -> 83.3 us
    dot_general x11 -> x0, matrix products: 238 us -> none  [the longest x5 97.6 us: block_update(): jnp.einsum('kgtj,jke->kgte', powers.astype(jnp.bfloat16), value_block, pr...]
    ppermute x12 -> x31, waiting for transfers between devices: 1.6 us -> 194 us  [the longest x12 191 us: flip(): return lax.ppermute(a, 'ctx', [(i, i ^ bit) for i in range(n_ctx)])]
    pallas_call x0 -> x12, Pallas kernels: none -> 107 us  [the longest x6 72.3 us: project(): pl.pallas_call(functools.partial(project_kernel, n_ctx=len(own), layout=l...]
    reduce_sum x5 -> x1, other arithmetic: 74.8 us -> 0.78 us  [steps(): jnp.sum((window_docs[None, :] < doc_ids[:, None]).astype(jnp.int32), axis...]
    all_gather x1 -> x0, waiting for transfers between devices: 33.6 us -> none  [local(): lax.all_gather(out_weight, ('ctx', 'dp'), axis=1, tiled=True)]
    ppermute x4 -> x0, local copies, waits for them, and re-layouts: 8.23 us -> none  [passed_along(): return lax.ppermute(block, axis, route)]
    ppermute x12 -> x31, starting transfers between devices: 75.7 us -> 83.3 us  [the longest x12 61.8 us: flip(): return lax.ppermute(a, 'ctx', [(i, i ^ bit) for i in range(n_ctx)])]
    unnamed x38 -> x40, local copies, waits for them, and re-layouts: 4.81 us -> 9.97 us
  transfers between devices with their start and end apart: 13 -> 31, of which waited for: 3 -> 11; matrix products, arithmetic and copies ran while one was open for 63% -> 1% of each run, Pallas kernels for 0% -> 24%
where the time goes in v1:
time: 402 us
  waiting for transfers between devices  194 us (48%)
  Pallas kernels  107 us (27%)
  starting transfers between devices  83.3 us (21%)
  local copies, waits for them, and re-layouts  10.8 us (3%)
  other arithmetic  6.06 us (2%)
    ppermute x12, waiting for transfers between devices, flip(): return lax.ppermute(a, 'ctx', [(i, i ^ bit) for i in range(n_ctx)])  191 us
    pallas_call x6, Pallas kernels, project(): pl.pallas_call(functools.partial(project_kernel, n_ctx=len(own), layout=l...  72.3 us
    ppermute x12, starting transfers between devices, flip(): return lax.ppermute(a, 'ctx', [(i, i ^ bit) for i in range(n_ctx)])  61.8 us
    pallas_call x4, Pallas kernels, attend(): pl.pallas_call(functools.partial(attend_kernel, heads=heads, tok=tok, q_t...  27.9 us
    ppermute x5, starting transfers between devices, rise(): return lax.ppermute(a, 'ctx', [(i, (i + by) % n_ctx) for i in range(n_ctx)])  14.7 us
    unnamed x40, local copies, waits for them, and re-layouts  9.97 us
  transfers between devices with their start and end apart: 31, of which 11 were waited for; matrix products, arithmetic and copies ran while one was open for 1% of the time, Pallas kernels for 24%

profile of v1, /device:TPU:0, one launch (start us, length us, event | category | flops | bytes accessed | tf_op | source)
XLA Modules:
  0.0 401.8 jit_solution(13699320969102967484)
XLA Ops:
  0.0 0.8 convert_element_type.26
  0.8 1.3 pad_maximum_fusion.refs_4_.refs_5_
  2.9 1.3 broadcast_select_fusion.1
  4.3 28.8 %collective-permute-start.1 = (bf16[528,1024]{1,0:T(8,128)(2,1)}, bf16[528,1024]{1,0:T(8,128)(2,1)S(1)}, u32[]{:S(2)}, u32[]{:S(2)}) collective-permute-start(bf16[528,1024]{1,0:T(8,128)(2,1)} %broadcast_select_fusion.1), channel_id=1, source_target_pairs={{0,4},{2,6},{4,0},{6,2},{8,12},{10,14},{12,8},{14,10},{16,20},{18,... | collective-permute-start | bytes 3244040 | tf_op jit(solution)/shard_map/ppermute | solution.py:296
  33.1 2.5 collective-permute-start.17
  35.6 22.4 %collective-permute-done.1.refs_0_.refs_1_ = bf16[528,1024]{1,0:T(8,128)(2,1)S(1)} collective-permute-done((bf16[528,1024]{1,0:T(8,128)(2,1)}, bf16[528,1024]{1,0:T(8,128)(2,1)S(1)}, u32[]{:S(2)}, u32[]{:S(2)}) %collective-permute-start.1) | collective-permute-done | bytes 1081376 | tf_op jit(solution)/shard_map/ppermute | solution.py:296
  58.0 1.3 broadcast_select_fusion
  59.3 1.5 collective-permute-start.2
  62.2 24.2 %collective-permute-done.2.refs_2_.refs_3_ = bf16[528,1024]{1,0:T(8,128)(2,1)} collective-permute-done((bf16[528,1024]{1,0:T(8,128)(2,1)}, bf16[528,1024]{1,0:T(8,128)(2,1)}, u32[]{:S(2)}, u32[]{:S(2)}) %collective-permute-start.2) | collective-permute-done | bytes 1081376 | tf_op jit(solution)/shard_map/ppermute | solution.py:296
  86.4 0.8 slice_bitcast_fusion.3
  87.2 14.2 %collective-permute-done.14.refs_10_ = bf16[4096,256]{1,0:T(8,128)(2,1)} collective-permute-done((bf16[4096,256]{1,0:T(8,128)(2,1)}, bf16[4096,256]{1,0:T(8,128)(2,1)}, u32[]{:S(2)}, u32[]{:S(2)}) %collective-permute-start.14) | collective-permute-done | bytes 2097184 | tf_op jit(solution)/shard_map/ppermute | solution.py:296
  101.3 4.5 %collective-permute-start.10 = (bf16[4096,256]{1,0:T(8,128)(2,1)}, bf16[4096,256]{1,0:T(8,128)(2,1)}, u32[]{:S(2)}, u32[]{:S(2)}) collective-permute-start(bf16[4096,256]{1,0:T(8,128)(2,1)} %refs_8_.1), channel_id=1, source_target_pairs={{0,24},{2,26},{4,28},{6,30},{8,0},{10,2},{12,4},{14,6},{16,8},{18,... | collective-permute-start | bytes 6291464 | tf_op jit(solution)/shard_map/ppermute | solution.py:299
  105.8 1.5 collective-permute-start.15
  108.7 1.8 collective-permute-start.19
  110.5 20.8 %collective-permute-done.13.refs_9_ = bf16[4096,256]{1,0:T(8,128)(2,1)} collective-permute-done((bf16[4096,256]{1,0:T(8,128)(2,1)}, bf16[4096,256]{1,0:T(8,128)(2,1)}, u32[]{:S(2)}, u32[]{:S(2)}) %collective-permute-start.13) | collective-permute-done | bytes 2097184 | tf_op jit(solution)/shard_map/ppermute | solution.py:296
  131.3 2.5 collective-permute-start.23
  133.8 0.8 convert_reduce_fusion
  135.0 2.2 copy-done
  137.2 6.8 %shard_map.67.refs_3_ = bf16[512,1024]{1,0:T(8,128)(2,1)S(1)} custom-call(s32[3]{0:T(128)S(1)} %pad_add_fusion.bounds_ref, bf16[512,4096]{1,0:T(8,128)(2,1)S(1)} %copy-done, s32[512,1]{1,0:T(8,128)S(1)} %copy.18.start_ref, s32[1,4096]{1,0:T(1,128)S(1)} %bitcast.58, bf16[528,1024]{1,0:T(8,128)(2,1)} %copy-done.2, bf16[528,1024]{1,0:T(8,128)(2,1)} %copy-done.2, ...), custom_call_target="tpu_custom_call" | custom-call | flops 4294967296 | bytes 2097152 | tf_op jit(solution)/shard_map/pallas_call | solution.py:99
  143.9 32.3 %collective-permute-done.15.refs_11_ = bf16[4096,256]{1,0:T(8,128)(2,1)} collective-permute-done((bf16[4096,256]{1,0:T(8,128)(2,1)}, bf16[4096,256]{1,0:T(8,128)(2,1)}, u32[]{:S(2)}, u32[]{:S(2)}) %collective-permute-start.15) | collective-permute-done | bytes 2097184 | tf_op jit(solution)/shard_map/ppermute | solution.py:296
  176.3 2.5 collective-permute-start.24
  178.8 6.8 %shard_map.66.refs_2_ = bf16[512,1024]{1,0:T(8,128)(2,1)S(1)} custom-call(s32[3]{0:T(128)S(1)} %pad_add_fusion.bounds_ref, bf16[512,4096]{1,0:T(8,128)(2,1)S(1)} %copy-done, s32[512,1]{1,0:T(8,128)S(1)} %copy.18.start_ref, s32[1,4096]{1,0:T(1,128)S(1)} %bitcast.59, bf16[528,1024]{1,0:T(8,128)(2,1)} %copy-done.2, bf16[528,1024]{1,0:T(8,128)(2,1)} %copy-done.2, ...), custom_call_target="tpu_custom_call" | custom-call | flops 4294967296 | bytes 2097152 | tf_op jit(solution)/shard_map/pallas_call | solution.py:99
  185.5 31.5 %collective-permute-done.18.refs_9_ = bf16[4096,256]{1,0:T(8,128)(2,1)} collective-permute-done((bf16[4096,256]{1,0:T(8,128)(2,1)}, bf16[4096,256]{1,0:T(8,128)(2,1)}, u32[]{:S(2)}, u32[]{:S(2)}) %collective-permute-start.18) | collective-permute-done | bytes 2097184 | tf_op jit(solution)/shard_map/ppermute | solution.py:296
  217.0 6.8 %shard_map.65.refs_1_ = bf16[512,1024]{1,0:T(8,128)(2,1)S(1)} custom-call(s32[3]{0:T(128)S(1)} %pad_add_fusion.bounds_ref, bf16[512,4096]{1,0:T(8,128)(2,1)S(1)} %copy-done, s32[512,1]{1,0:T(8,128)S(1)} %copy.18.start_ref, s32[1,4096]{1,0:T(1,128)S(1)} %bitcast.60, bf16[528,1024]{1,0:T(8,128)(2,1)} %copy-done.2, bf16[528,1024]{1,0:T(8,128)(2,1)} %copy-done.2, ...), custom_call_target="tpu_custom_call" | custom-call | flops 4294967296 | bytes 2097152 | tf_op jit(solution)/shard_map/pallas_call | solution.py:99
  223.8 4.9 %collective-permute-start.11 = (bf16[4096,256]{1,0:T(8,128)(2,1)}, bf16[4096,256]{1,0:T(8,128)(2,1)}, u32[]{:S(2)}, u32[]{:S(2)}) collective-permute-start(bf16[4096,256]{1,0:T(8,128)(2,1)} %collective-permute-done.10.refs_8_), channel_id=1, source_target_pairs={{0,2},{2,0},{4,6},{6,4},{8,10},{10,8},{12,14},{14,12},{16,18},{18,... | collective-permute-start | bytes 6291464 | tf_op jit(solution)/shard_map/ppermute | solution.py:296
  228.8 3.6 collective-permute-start.7
  232.4 7.6 %shard_map.64.refs_0_ = bf16[512,1024]{1,0:T(8,128)(2,1)} custom-call(s32[3]{0:T(128)S(1)} %pad_add_fusion.bounds_ref, bf16[512,4096]{1,0:T(8,128)(2,1)S(1)} %copy-done, s32[512,1]{1,0:T(8,128)S(1)} %copy.18.start_ref, s32[1,4096]{1,0:T(1,128)S(1)} %bitcast.61, bf16[528,1024]{1,0:T(8,128)(2,1)} %copy-done.2, bf16[528,1024]{1,0:T(8,128)(2,1)} %copy-done.2, ...), custom_call_target="tpu_custom_call" | custom-call | flops 4294967296 | bytes 2097152 | tf_op jit(solution)/shard_map/pallas_call | solution.py:99
  239.9 1.8 collective-permute-start.6
  241.7 1.0 copy-done.8
  242.7 12.5 %collective-permute-start.21 = (bf16[4096,256]{1,0:T(8,128)(2,1)}, bf16[4096,256]{1,0:T(8,128)(2,1)}, u32[]{:S(2)}, u32[]{:S(2)}) collective-permute-start(bf16[4096,256]{1,0:T(8,128)(2,1)} %collective-permute-done.10.refs_8_), channel_id=1, source_target_pairs={{0,4},{2,6},{4,0},{6,2},{8,12},{10,14},{12,8},{14,10},{16,20},{18,... | collective-permute-start | bytes 6291464 | tf_op jit(solution)/shard_map/ppermute | solution.py:296
  255.7 2.8 collective-permute-start.28
  258.5 16.2 %shard_map.68 = (bf16[512,8192]{1,0:T(8,128)(2,1)}, bf16[512,1024]{1,0:T(8,128)(2,1)}) custom-call(s32[4]{0:T(128)S(1)} %pad_add_fusion.1.idx_ref, bf16[512,1024]{1,0:T(8,128)(2,1)} %shard_map.64.refs_0_, bf16[512,1024]{1,0:T(8,128)(2,1)S(1)} %shard_map.65.refs_1_, bf16[512,1024]{1,0:T(8,128)(2,1)S(1)} %shard_map.66.refs_2_, ...), custom_call_target="tpu_custom_call" | custom-call | flops 8589934592 | bytes 16777216 | tf_op jit(solution)/shard_map/pallas_call | solution.py:202
  274.6 9.6 %collective-permute-start.12 = (bf16[4096,256]{1,0:T(8,128)(2,1)}, bf16[4096,256]{1,0:T(8,128)(2,1)}, u32[]{:S(2)}, u32[]{:S(2)}) collective-permute-start(bf16[4096,256]{1,0:T(8,128)(2,1)} %collective-permute-done.11.refs_9_), channel_id=1, source_target_pairs={{0,4},{2,6},{4,0},{6,2},{8,12},{10,14},{12,8},{14,10},{16,20},{18,... | collective-permute-start | bytes 6291464 | tf_op jit(solution)/shard_map/ppermute | solution.py:296
  284.3 13.1 %shard_map.69 = (bf16[512,8192]{1,0:T(8,128)(2,1)}, bf16[512,768]{1,0:T(8,128)(2,1)}) custom-call(s32[3]{0:T(128)S(1)} %pad_add_fusion.2.idx_ref, bf16[512,1024]{1,0:T(8,128)(2,1)} %shard_map.64.refs_0_, bf16[512,1024]{1,0:T(8,128)(2,1)S(1)} %shard_map.65.refs_1_, bf16[512,1024]{1,0:T(8,128)(2,1)S(1)} %shard_map.66.refs_2_, ...), custom_call_target="tpu_custom_call", output_to_operand_aliasing={{0}: (12, {})} | custom-call | flops 6442450944 | bytes 14680064 | tf_op jit(solution)/shard_map/pallas_call | solution.py:202
  297.4 4.7 %collective-permute-done.21.refs_10_ = bf16[4096,256]{1,0:T(8,128)(2,1)} collective-permute-done((bf16[4096,256]{1,0:T(8,128)(2,1)}, bf16[4096,256]{1,0:T(8,128)(2,1)}, u32[]{:S(2)}, u32[]{:S(2)}) %collective-permute-start.21) | collective-permute-done | bytes 2097184 | tf_op jit(solution)/shard_map/ppermute | solution.py:296
  302.0 13.0 %shard_map.70 = (bf16[512,8192]{1,0:T(8,128)(2,1)}, bf16[512,768]{1,0:T(8,128)(2,1)S(1)}) custom-call(s32[3]{0:T(128)S(1)} %pad_add_fusion.3.idx_ref, bf16[512,1024]{1,0:T(8,128)(2,1)} %shard_map.64.refs_0_, bf16[512,1024]{1,0:T(8,128)(2,1)S(1)} %shard_map.65.refs_1_, bf16[512,1024]{1,0:T(8,128)(2,1)S(1)} %shard_map.66.refs_2_, ...), custom_call_target="tpu_custom_call", output_to_operand_aliasing={{0}: (12, {})} | custom-call | flops 6442450944 | bytes 14680064 | tf_op jit(solution)/shard_map/pallas_call | solution.py:202
  315.1 31.8 %collective-permute-done.25.refs_10_ = bf16[4096,256]{1,0:T(8,128)(2,1)S(1)} collective-permute-done((bf16[4096,256]{1,0:T(8,128)(2,1)}, bf16[4096,256]{1,0:T(8,128)(2,1)S(1)}, u32[]{:S(2)}, u32[]{:S(2)}) %collective-permute-start.25) | collective-permute-done | bytes 2097184 | tf_op jit(solution)/shard_map/ppermute | solution.py:296
  346.9 1.4 copy-done.14
  348.2 13.3 %shard_map.71 = (bf16[512,8192]{1,0:T(8,128)(2,1)}, bf16[512,768]{1,0:T(8,128)(2,1)}) custom-call(s32[3]{0:T(128)S(1)} %pad_add_fusion.4.idx_ref, bf16[512,1024]{1,0:T(8,128)(2,1)} %shard_map.64.refs_0_, bf16[512,1024]{1,0:T(8,128)(2,1)S(1)} %shard_map.65.refs_1_, bf16[512,1024]{1,0:T(8,128)(2,1)S(1)} %shard_map.66.refs_2_, ...), custom_call_target="tpu_custom_call", output_to_operand_aliasing={{0}: (12, {})} | custom-call | flops 6442450944 | bytes 14680064 | tf_op jit(solution)/shard_map/pallas_call | solution.py:202
  362.2 0.8 copy-done.9
  363.6 10.0 %shard_map.72 = (bf16[512,8192]{1,0:T(8,128)(2,1)}, bf16[512,512]{1,0:T(8,128)(2,1)}) custom-call(s32[2]{0:T(128)S(1)} %pad_add_fusion.5.idx_ref, bf16[512,1024]{1,0:T(8,128)(2,1)} %shard_map.64.refs_0_, bf16[512,1024]{1,0:T(8,128)(2,1)S(1)} %shard_map.65.refs_1_, bf16[512,1024]{1,0:T(8,128)(2,1)S(1)} %shard_map.66.refs_2_, ...), custom_call_target="tpu_custom_call", output_to_operand_aliasing={{0}: (11, {})} | custom-call | flops 4294967296 | bytes 12582912 | tf_op jit(solution)/shard_map/pallas_call | solution.py:202
  373.6 0.9 copy-done.11
  375.1 1.6 collective-permute-done.29.refs_4_
  376.8 4.8 %shard_map.73.refs_9_ = bf16[512,8192]{1,0:T(8,128)(2,1)} custom-call(s32[15]{0:T(128)} %stack.131.idx_ref, bf16[512,1024]{1,0:T(8,128)(2,1)} %collective-permute-done.16.refs_0_, bf16[512,768]{1,0:T(8,128)(2,1)} %collective-permute-done.20.refs_1_, bf16[512,768]{1,0:T(8,128)(2,1)} %copy-done.11, ...), custom_call_target="tpu_custom_call", output_to_operand_aliasing={{}: (6, {})} | custom-call | tf_op jit(solution)/shard_map/pallas_call | solution.py:261
  381.6 9.3 %collective-permute-done.12.refs_8_ = bf16[4096,256]{1,0:T(8,128)(2,1)} collective-permute-done((bf16[4096,256]{1,0:T(8,128)(2,1)}, bf16[4096,256]{1,0:T(8,128)(2,1)}, u32[]{:S(2)}, u32[]{:S(2)}) %collective-permute-start.12) | collective-permute-done | bytes 2097184 | tf_op jit(solution)/shard_map/ppermute | solution.py:296
  390.9 6.7 %shard_map.74 = (bf16[512,8192]{1,0:T(8,128)(2,1)}, bf16[512,256]{1,0:T(8,128)(2,1)S(1)}) custom-call(s32[1]{0:T(128)} %bitcast.1.idx_ref, bf16[512,1024]{1,0:T(8,128)(2,1)} %shard_map.64.refs_0_, bf16[512,1024]{1,0:T(8,128)(2,1)S(1)} %shard_map.65.refs_1_, bf16[512,1024]{1,0:T(8,128)(2,1)S(1)} %shard_map.66.refs_2_, ...), custom_call_target="tpu_custom_call", output_to_operand_aliasing={{0}: (10, {})} | custom-call | flops 2147483648 | bytes 10485760 | tf_op jit(solution)/shard_map/pallas_call | solution.py:202
  397.7 1.5 collective-permute-done.30.refs_0_
  399.9 1.7 shard_map.75
  (90 shorter events, 7.0 us)
Async XLA Ops:
  0.0 2.9 copy-start.6
  0.0 2.9 copy-start.5
  2.1 57.2 %copy-start.3 = (bf16[528,1024]{1,0:T(8,128)(2,1)}, bf16[528,1024]{1,0:T(8,128)(2,1)S(1)}, u32[]{:S(2)}) copy-start(bf16[528,1024]{1,0:T(8,128)(2,1)S(1)} %pad_maximum_fusion.refs_4_.refs_5_) | copy-start | bytes 3244036
  2.1 0.8 collective-permute-start
  4.3 104.4 %copy-start.13 = (s32[512]{0:T(512)S(1)}, s32[512]{0:T(512)}, u32[]{:S(2)}) copy-start(s32[512]{0:T(512)} %param.9) | copy-start | bytes 6148
  4.3 53.7 %collective-permute-start.1 = (bf16[528,1024]{1,0:T(8,128)(2,1)}, bf16[528,1024]{1,0:T(8,128)(2,1)S(1)}, u32[]{:S(2)}, u32[]{:S(2)}) collective-permute-start(bf16[528,1024]{1,0:T(8,128)(2,1)} %broadcast_select_fusion.1), channel_id=1, source_target_pairs={{0,4},{2,6},{4,0},{6,2},{8,12},{10,14},{12,8},{14,10},{16,20},{18,... | collective-permute-start | bytes 3244040 | tf_op jit(solution)/shard_map/ppermute | solution.py:296
  33.1 68.3 %collective-permute-start.14 = (bf16[4096,256]{1,0:T(8,128)(2,1)}, bf16[4096,256]{1,0:T(8,128)(2,1)}, u32[]{:S(2)}, u32[]{:S(2)}) collective-permute-start(bf16[4096,256]{1,0:T(8,128)(2,1)} %refs_8_.1), channel_id=1, source_target_pairs={{0,4},{2,6},{4,0},{6,2},{8,12},{10,14},{12,8},{14,10},{16,20},{18,... | collective-permute-start | bytes 6291464 | tf_op jit(solution)/shard_map/ppermute | solution.py:296
  33.1 72.7 %collective-permute-start.17 = (bf16[4096,256]{1,0:T(8,128)(2,1)}, bf16[4096,256]{1,0:T(8,128)(2,1)}, u32[]{:S(2)}, u32[]{:S(2)}) collective-permute-start(bf16[4096,256]{1,0:T(8,128)(2,1)} %refs_8_.1), channel_id=1, source_target_pairs={{0,8},{2,10},{4,12},{6,14},{8,16},{10,18},{12,20},{14,22},{16,24},... | collective-permute-start | bytes 6291464 | tf_op jit(solution)/shard_map/ppermute | solution.py:299
  35.6 25.3 %collective-permute-start.5 = (bf16[528,1024]{1,0:T(8,128)(2,1)S(1)}, bf16[528,1024]{1,0:T(8,128)(2,1)}, u32[]{:S(2)}, u32[]{:S(2)}) collective-permute-start(bf16[528,1024]{1,0:T(8,128)(2,1)S(1)} %pad_maximum_fusion.refs_4_.refs_5_), channel_id=1, source_target_pairs={{0,1},{1,0},{2,3},{3,2},{4,5},{5,4},{6,7},{7,6},{8,9},{9,8},{10,11... | collective-permute-start | bytes 3244040 | tf_op jit(solution)/shard_map/ppermute | solution.py:289
  35.6 99.4 %copy-start.1 = (s32[4096]{0:T(1024)S(1)}, s32[4096]{0:T(1024)}, u32[]{:S(2)}) copy-start(s32[4096]{0:T(1024)} %param.10) | copy-start | bytes 49156
  58.0 76.8 %copy-start.2 = (bf16[528,1024]{1,0:T(8,128)(2,1)}, bf16[528,1024]{1,0:T(8,128)(2,1)S(1)}, u32[]{:S(2)}) copy-start(bf16[528,1024]{1,0:T(8,128)(2,1)S(1)} %collective-permute-done.1.refs_0_.refs_1_) | copy-start | bytes 3244036
  59.3 27.1 %collective-permute-start.2 = (bf16[528,1024]{1,0:T(8,128)(2,1)}, bf16[528,1024]{1,0:T(8,128)(2,1)}, u32[]{:S(2)}, u32[]{:S(2)}) collective-permute-start(bf16[528,1024]{1,0:T(8,128)(2,1)} %broadcast_select_fusion), channel_id=1, source_target_pairs={{0,2},{2,0},{4,6},{6,4},{8,10},{10,8},{12,14},{14,12},{16,18},{18,... | collective-permute-start | bytes 3244040 | tf_op jit(solution)/shard_map/ppermute | solution.py:296
  60.8 46.5 %collective-permute-start.3 = (bf16[528,1024]{1,0:T(8,128)(2,1)S(1)}, bf16[528,1024]{1,0:T(8,128)(2,1)}, u32[]{:S(2)}, u32[]{:S(2)}) collective-permute-start(bf16[528,1024]{1,0:T(8,128)(2,1)S(1)} %collective-permute-done.1.refs_0_.refs_1_), channel_id=1, source_target_pairs={{0,1},{1,0},{2,3},{3,2},{4,5},{5,4},{6,7},{7,6},{8,9},{9,8},{10,11... | collective-permute-start | bytes 3244040 | tf_op jit(solution)/shard_map/ppermute | solution.py:289
  60.8 70.5 %collective-permute-start.13 = (bf16[4096,256]{1,0:T(8,128)(2,1)}, bf16[4096,256]{1,0:T(8,128)(2,1)}, u32[]{:S(2)}, u32[]{:S(2)}) collective-permute-start(bf16[4096,256]{1,0:T(8,128)(2,1)} %refs_8_.1), channel_id=1, source_target_pairs={{0,2},{2,0},{4,6},{6,4},{8,10},{10,8},{12,14},{14,12},{16,18},{18,... | collective-permute-start | bytes 6291464 | tf_op jit(solution)/shard_map/ppermute | solution.py:296
  86.4 22.3 %collective-permute-start.4 = (bf16[528,1024]{1,0:T(8,128)(2,1)}, bf16[528,1024]{1,0:T(8,128)(2,1)S(1)}, u32[]{:S(2)}, u32[]{:S(2)}) collective-permute-start(bf16[528,1024]{1,0:T(8,128)(2,1)} %collective-permute-done.2.refs_2_.refs_3_), channel_id=1, source_target_pairs={{0,1},{1,0},{2,3},{3,2},{4,5},{5,4},{6,7},{7,6},{8,9},{9,8},{10,11... | collective-permute-start | bytes 3244040 | tf_op jit(solution)/shard_map/ppermute | solution.py:289
  101.3 77.4 %collective-permute-start.10 = (bf16[4096,256]{1,0:T(8,128)(2,1)}, bf16[4096,256]{1,0:T(8,128)(2,1)}, u32[]{:S(2)}, u32[]{:S(2)}) collective-permute-start(bf16[4096,256]{1,0:T(8,128)(2,1)} %refs_8_.1), channel_id=1, source_target_pairs={{0,24},{2,26},{4,28},{6,30},{8,0},{10,2},{12,4},{14,6},{16,8},{18,... | collective-permute-start | bytes 6291464 | tf_op jit(solution)/shard_map/ppermute | solution.py:299
  105.8 70.4 %collective-permute-start.15 = (bf16[4096,256]{1,0:T(8,128)(2,1)}, bf16[4096,256]{1,0:T(8,128)(2,1)}, u32[]{:S(2)}, u32[]{:S(2)}) collective-permute-start(bf16[4096,256]{1,0:T(8,128)(2,1)} %collective-permute-done.14.refs_10_), channel_id=1, source_target_pairs={{0,2},{2,0},{4,6},{6,4},{8,10},{10,8},{12,14},{14,12},{16,18},{18,... | collective-permute-start | bytes 6291464 | tf_op jit(solution)/shard_map/ppermute | solution.py:296
  107.3 109.7 %collective-permute-start.18 = (bf16[4096,256]{1,0:T(8,128)(2,1)}, bf16[4096,256]{1,0:T(8,128)(2,1)}, u32[]{:S(2)}, u32[]{:S(2)}) collective-permute-start(bf16[4096,256]{1,0:T(8,128)(2,1)} %collective-permute-done.17.refs_8_), channel_id=1, source_target_pairs={{0,2},{2,0},{4,6},{6,4},{8,10},{10,8},{12,14},{14,12},{16,18},{18,... | collective-permute-start | bytes 6291464 | tf_op jit(solution)/shard_map/ppermute | solution.py:296
  108.7 25.9 %copy-start.4 = (bf16[528,1024]{1,0:T(8,128)(2,1)}, bf16[528,1024]{1,0:T(8,128)(2,1)S(1)}, u32[]{:S(2)}) copy-start(bf16[528,1024]{1,0:T(8,128)(2,1)S(1)} %collective-permute-done.4.refs_8_.refs_9_) | copy-start | bytes 3244036
  108.7 115.1 %collective-permute-start.19 = (bf16[4096,256]{1,0:T(8,128)(2,1)}, bf16[4096,256]{1,0:T(8,128)(2,1)}, u32[]{:S(2)}, u32[]{:S(2)}) collective-permute-start(bf16[4096,256]{1,0:T(8,128)(2,1)} %collective-permute-done.17.refs_8_), channel_id=1, source_target_pairs={{0,4},{2,6},{4,0},{6,2},{8,12},{10,14},{12,8},{14,10},{16,20},{18,... | collective-permute-start | bytes 6291464 | tf_op jit(solution)/shard_map/ppermute | solution.py:296
  131.3 97.4 %collective-permute-start.23 = (bf16[4096,256]{1,0:T(8,128)(2,1)}, bf16[4096,256]{1,0:T(8,128)(2,1)}, u32[]{:S(2)}, u32[]{:S(2)}) collective-permute-start(bf16[4096,256]{1,0:T(8,128)(2,1)} %collective-permute-done.17.refs_8_), channel_id=1, source_target_pairs={{0,8},{2,10},{4,12},{6,14},{8,16},{10,18},{12,20},{14,22},{16,24},... | collective-permute-start | bytes 6291464 | tf_op jit(solution)/shard_map/ppermute | solution.py:299
  135.0 2.2 copy-start
  176.3 79.4 %collective-permute-start.24 = (bf16[4096,256]{1,0:T(8,128)(2,1)}, bf16[4096,256]{1,0:T(8,128)(2,1)}, u32[]{:S(2)}, u32[]{:S(2)}) collective-permute-start(bf16[4096,256]{1,0:T(8,128)(2,1)} %collective-permute-done.15.refs_11_), channel_id=1, source_target_pairs={{0,8},{2,10},{4,12},{6,14},{8,16},{10,18},{12,20},{14,22},{16,24},... | collective-permute-start | bytes 6291464 | tf_op jit(solution)/shard_map/ppermute | solution.py:299
  178.8 61.2 %collective-permute-start.9 = (bf16[512,1024]{1,0:T(8,128)(2,1)S(1)}, bf16[512,1024]{1,0:T(8,128)(2,1)S(1)}, u32[]{:S(2)}, u32[]{:S(2)}) collective-permute-start(bf16[512,1024]{1,0:T(8,128)(2,1)S(1)} %shard_map.67.refs_3_), channel_id=1, source_target_pairs={{0,1},{1,0},{2,3},{3,2},{4,5},{5,4},{6,7},{7,6},{8,9},{9,8},{10,11... | collective-permute-start | bytes 3145736 | tf_op jit(solution)/shard_map/ppermute | solution.py:289
  217.0 24.6 %collective-permute-start.8 = (bf16[512,1024]{1,0:T(8,128)(2,1)S(1)}, bf16[512,1024]{1,0:T(8,128)(2,1)S(1)}, u32[]{:S(2)}, u32[]{:S(2)}) collective-permute-start(bf16[512,1024]{1,0:T(8,128)(2,1)S(1)} %shard_map.66.refs_2_), channel_id=1, source_target_pairs={{0,1},{1,0},{2,3},{3,2},{4,5},{5,4},{6,7},{7,6},{8,9},{9,8},{10,11... | collective-permute-start | bytes 3145736 | tf_op jit(solution)/shard_map/ppermute | solution.py:289
  223.8 50.8 %collective-permute-start.11 = (bf16[4096,256]{1,0:T(8,128)(2,1)}, bf16[4096,256]{1,0:T(8,128)(2,1)}, u32[]{:S(2)}, u32[]{:S(2)}) collective-permute-start(bf16[4096,256]{1,0:T(8,128)(2,1)} %collective-permute-done.10.refs_8_), channel_id=1, source_target_pairs={{0,2},{2,0},{4,6},{6,4},{8,10},{10,8},{12,14},{14,12},{16,18},{18,... | collective-permute-start | bytes 6291464 | tf_op jit(solution)/shard_map/ppermute | solution.py:296
  228.8 26.8 %collective-permute-start.7 = (bf16[512,1024]{1,0:T(8,128)(2,1)S(1)}, bf16[512,1024]{1,0:T(8,128)(2,1)}, u32[]{:S(2)}, u32[]{:S(2)}) collective-permute-start(bf16[512,1024]{1,0:T(8,128)(2,1)S(1)} %shard_map.65.refs_1_), channel_id=1, source_target_pairs={{0,1},{1,0},{2,3},{3,2},{4,5},{5,4},{6,7},{7,6},{8,9},{9,8},{10,11... | collective-permute-start | bytes 3145736 | tf_op jit(solution)/shard_map/ppermute | solution.py:289
  239.9 1.8 copy-start.7
  239.9 15.7 %collective-permute-start.6 = (bf16[512,1024]{1,0:T(8,128)(2,1)}, bf16[512,1024]{1,0:T(8,128)(2,1)}, u32[]{:S(2)}, u32[]{:S(2)}) collective-permute-start(bf16[512,1024]{1,0:T(8,128)(2,1)} %shard_map.64.refs_0_), channel_id=1, source_target_pairs={{0,1},{1,0},{2,3},{3,2},{4,5},{5,4},{6,7},{7,6},{8,9},{9,8},{10,11... | collective-permute-start | bytes 3145736 | tf_op jit(solution)/shard_map/ppermute | solution.py:289
  241.7 1.0 copy-start.8
  242.7 59.3 %collective-permute-start.21 = (bf16[4096,256]{1,0:T(8,128)(2,1)}, bf16[4096,256]{1,0:T(8,128)(2,1)}, u32[]{:S(2)}, u32[]{:S(2)}) collective-permute-start(bf16[4096,256]{1,0:T(8,128)(2,1)} %collective-permute-done.10.refs_8_), channel_id=1, source_target_pairs={{0,4},{2,6},{4,0},{6,2},{8,12},{10,14},{12,8},{14,10},{16,20},{18,... | collective-permute-start | bytes 6291464 | tf_op jit(solution)/shard_map/ppermute | solution.py:296
  255.6 91.3 %collective-permute-start.25 = (bf16[4096,256]{1,0:T(8,128)(2,1)}, bf16[4096,256]{1,0:T(8,128)(2,1)S(1)}, u32[]{:S(2)}, u32[]{:S(2)}) collective-permute-start(bf16[4096,256]{1,0:T(8,128)(2,1)} %collective-permute-done.23.refs_8_), channel_id=1, source_target_pairs={{0,4},{2,6},{4,0},{6,2},{8,12},{10,14},{12,8},{14,10},{16,20},{18,... | collective-permute-start | bytes 6291464 | tf_op jit(solution)/shard_map/ppermute | solution.py:296
  255.7 105.9 %collective-permute-start.27 = (bf16[4096,256]{1,0:T(8,128)(2,1)}, bf16[4096,256]{1,0:T(8,128)(2,1)S(1)}, u32[]{:S(2)}, u32[]{:S(2)}) collective-permute-start(bf16[4096,256]{1,0:T(8,128)(2,1)} %collective-permute-done.23.refs_8_), channel_id=1, source_target_pairs={{0,2},{2,0},{4,6},{6,4},{8,10},{10,8},{12,14},{14,12},{16,18},{18,... | collective-permute-start | bytes 6291464 | tf_op jit(solution)/shard_map/ppermute | solution.py:296
  255.7 106.0 %collective-permute-start.28 = (bf16[4096,256]{1,0:T(8,128)(2,1)}, bf16[4096,256]{1,0:T(8,128)(2,1)S(1)}, u32[]{:S(2)}, u32[]{:S(2)}) collective-permute-start(bf16[4096,256]{1,0:T(8,128)(2,1)} %collective-permute-done.24.refs_9_), channel_id=1, source_target_pairs={{0,8},{2,10},{4,12},{6,14},{8,16},{10,18},{12,20},{14,22},{16,24},... | collective-permute-start | bytes 6291464 | tf_op jit(solution)/shard_map/ppermute | solution.py:299
  274.6 116.2 %collective-permute-start.12 = (bf16[4096,256]{1,0:T(8,128)(2,1)}, bf16[4096,256]{1,0:T(8,128)(2,1)}, u32[]{:S(2)}, u32[]{:S(2)}) collective-permute-start(bf16[4096,256]{1,0:T(8,128)(2,1)} %collective-permute-done.11.refs_9_), channel_id=1, source_target_pairs={{0,4},{2,6},{4,0},{6,2},{8,12},{10,14},{12,8},{14,10},{16,20},{18,... | collective-permute-start | bytes 6291464 | tf_op jit(solution)/shard_map/ppermute | solution.py:296
  315.0 58.6 %collective-permute-start.22 = (bf16[512,768]{1,0:T(8,128)(2,1)S(1)}, bf16[512,768]{1,0:T(8,128)(2,1)S(1)}, u32[]{:S(2)}, u32[]{:S(2)}) collective-permute-start(bf16[512,768]{1,0:T(8,128)(2,1)S(1)} %get-tuple-element.21), channel_id=1, source_target_pairs={{0,1},{1,0},{2,3},{3,2},{4,5},{5,4},{6,7},{7,6},{8,9},{9,8},{10,11... | collective-permute-start | bytes 2359304 | tf_op jit(solution)/shard_map/ppermute | solution.py:289
  346.9 1.4 copy-start.14
  346.9 28.3 %collective-permute-start.16 = (bf16[512,1024]{1,0:T(8,128)(2,1)}, bf16[512,1024]{1,0:T(8,128)(2,1)}, u32[]{:S(2)}, u32[]{:S(2)}) collective-permute-start(bf16[512,1024]{1,0:T(8,128)(2,1)} %get-tuple-element.17), channel_id=1, source_target_pairs={{0,1},{1,0},{2,3},{3,2},{4,5},{5,4},{6,7},{7,6},{8,9},{9,8},{10,11... | collective-permute-start | bytes 3145736 | tf_op jit(solution)/shard_map/ppermute | solution.py:289
  361.6 1.4 copy-start.9
  361.6 13.5 %collective-permute-start.20 = (bf16[512,768]{1,0:T(8,128)(2,1)}, bf16[512,768]{1,0:T(8,128)(2,1)}, u32[]{:S(2)}, u32[]{:S(2)}) collective-permute-start(bf16[512,768]{1,0:T(8,128)(2,1)} %get-tuple-element.19), channel_id=1, source_target_pairs={{0,1},{1,0},{2,3},{3,2},{4,5},{5,4},{6,7},{7,6},{8,9},{9,8},{10,11... | collective-permute-start | bytes 2359304 | tf_op jit(solution)/shard_map/ppermute | solution.py:289
  361.7 1.9 copy-start.10
  361.7 13.4 %collective-permute-start.26 = (bf16[512,768]{1,0:T(8,128)(2,1)}, bf16[512,768]{1,0:T(8,128)(2,1)}, u32[]{:S(2)}, u32[]{:S(2)}) collective-permute-start(bf16[512,768]{1,0:T(8,128)(2,1)} %get-tuple-element.23), channel_id=1, source_target_pairs={{0,1},{1,0},{2,3},{3,2},{4,5},{5,4},{6,7},{7,6},{8,9},{9,8},{10,11... | collective-permute-start | bytes 2359304 | tf_op jit(solution)/shard_map/ppermute | solution.py:289
  373.6 0.9 copy-start.11
  374.5 2.3 collective-permute-start.29
  397.6 1.6 collective-permute-start.30
  399.2 0.7 copy-start.12
